TPU v7x, 32 devices: a whole 2x2x4 slice. The times are simulated.
32 devices in a mesh: seq: 8 (over z, x), tp: 4 (over y, core).
Axes of the slice: x: 2, y: 2, z: 4, core: 2. Of those that a mesh axis runs over, the one named last changes fastest.
Arguments:
- hidden: bfloat16 [2048, 8192], P('seq', 'tp'), may hold values from -6 to 6
- norm_gain: float32 [8192], replicated, may hold values from 0.1 to 1.9
- w_query: bfloat16 [8192, 4096], P('seq', 'tp')
- w_key: bfloat16 [8192, 512], P('seq', 'tp')
- value_weight: bfloat16 [8192, 512], P('seq', 'tp'), may hold values from -0.0625 to 0.0625
- vertical_blocks: int32 [32, 16], replicated, may hold values from 0 to 31, as said below
- slash_offsets: int32 [32, 16], replicated, may hold values from 0 to 31, as said below
- counts: int32 [32, 2], replicated, may hold values from 1 to 16, as said below
Outputs:
- attn_out: bfloat16 [2048, 4096], P('seq', 'tp')
- key_value_cache: bfloat16 [2, 2048, 512], P(None, 'seq', 'tp')
Inputs may be any that keep to these rules, and one draw needn't show every extreme that they name: `vertical_blocks`: the 16 entries of a head are distinct block indices; only the first counts[j, 0] of row j are used. `slash_offsets`: the 16 entries of a head are distinct block offsets, the first of them 0; only the first counts[j, 1] of row j are used. `counts`: column 0 is the number of used vertical blocks, column 1 the number of used slash offsets; some head uses all 16 and all 16.
All inputs are finite; a program needn't handle non-finite values.
Results may differ from a plain program's by a relative error of at most 0.0079.
Values may be sent and summed in bfloat16 or wider, within the bound.
No kernel may reach another device: no remote copies, remote signals or barrier semaphores. Data moves between devices by JAX's collectives and lax.ppermute only.
A program may use at most 128 MiB of HBM per device.

v0:
```python
import jax
import jax.numpy as jnp
from jax import lax
from jax.sharding import PartitionSpec as P

BLOCK = 64
EPSILON = 1e-06
THETA = 1000000.0
NEGATIVE = -1e30


def apply_rotary(value_rows, token_positions, head_width):
    half_width = head_width // 2
    inv_freq = THETA ** (-(jnp.arange(half_width, dtype=jnp.float32) * 2.0) / head_width)
    angles = token_positions.astype(jnp.float32)[:, None] * inv_freq[None, :]
    cosine = jnp.cos(angles)[:, None, :]
    sine_wave = jnp.sin(angles)[:, None, :]
    first_half = value_rows[..., :half_width]
    second = value_rows[..., half_width:]
    return jnp.concatenate(
        [first_half * cosine - second * sine_wave, second * cosine + first_half * sine_wave],
        axis=-1,
    )


def lookup(table_values, head_ids):
    matches = head_ids[:, None] == jnp.arange(table_values.shape[0], dtype=jnp.int32)[None, :]
    return jnp.sum(jnp.where(matches[:, :, None], table_values[None, :, :], 0), axis=1)


def candidates(blocks, head_ids, vertical_blocks, slash_offsets, counts):
    verticals = lookup(vertical_blocks, head_ids)
    slashes = lookup(slash_offsets, head_ids)
    used = lookup(counts, head_ids)
    slash_live = jnp.arange(slashes.shape[1], dtype=jnp.int32)[None, :] < used[:, 1:2]
    slash_rows = blocks[:, None] - slashes
    slash_ok = slash_live & (slash_rows >= 0)
    repeated = jnp.any(
        (blocks[:, None, None] - verticals[:, :, None] == slashes[:, None, :])
        & slash_live[:, None, :],
        axis=2,
    )
    vertical_ok = (
        jnp.arange(verticals.shape[1], dtype=jnp.int32)[None, :] < used[:, 0:1]
    ) & jnp.logical_not(repeated)
    key_blocks = jnp.concatenate([verticals, jnp.maximum(slash_rows, 0)], axis=1)
    block_live = jnp.concatenate([vertical_ok, slash_ok], axis=1)
    return (key_blocks, block_live)


def attend(queries, starts, head_ids, block_table, vertical_blocks, slash_offsets, counts):
    unit_count, row_count, head_width = queries.shape
    key_blocks, block_live = candidates(
        starts // BLOCK, head_ids, vertical_blocks, slash_offsets, counts
    )
    offsets = jnp.arange(BLOCK, dtype=jnp.int32)
    key_pos = (key_blocks[:, :, None] * BLOCK + offsets[None, None, :]).reshape(unit_count, -1)
    key_live = jnp.repeat(block_live, BLOCK, axis=1)
    query_pos = starts[:, None] + jnp.arange(row_count, dtype=jnp.int32)[None, :]
    allowed = key_live[:, None, :] & (key_pos[:, None, :] <= query_pos[:, :, None])
    picked = jnp.take(block_table, key_blocks, axis=0).reshape(unit_count, -1, 2 * head_width)
    picked_keys = picked[:, :, :head_width]
    picked_values = picked[:, :, head_width:]
    scores = jnp.einsum(
        "uqd,ukd->uqk", queries, picked_keys, preferred_element_type=jnp.float32
    ) * head_width ** (-0.5)
    masked = jnp.where(allowed, scores, NEGATIVE)
    row_max = jnp.max(masked, axis=-1, keepdims=True)
    weights = jnp.where(allowed, jnp.exp(masked - row_max), 0.0)
    row_sum = jnp.sum(weights, axis=-1, keepdims=True)
    blended = jnp.einsum(
        "uqk,ukd->uqd",
        weights.astype(jnp.bfloat16),
        picked_values,
        preferred_element_type=jnp.float32,
    )
    return (blended / row_sum).astype(jnp.bfloat16)


def attend_all(
    queries, starts, head_ids, keys_all, values_all, vertical_blocks, slash_offsets, counts
):
    unit_count, unit_rows, head_width = queries.shape
    group_units = max(1, min(unit_count, 512 // unit_rows))
    step_count = unit_count // group_units
    block_table = jnp.concatenate([keys_all, values_all], axis=1).reshape(-1, BLOCK, 2 * head_width)

    def one_group(packed):
        return attend(
            packed[0], packed[1], packed[2], block_table, vertical_blocks, slash_offsets, counts
        )

    result = lax.map(
        one_group,
        (
            queries.reshape(step_count, group_units, unit_rows, head_width),
            starts.reshape(step_count, group_units),
            head_ids.reshape(step_count, group_units),
        ),
    )
    return result.reshape(unit_count, unit_rows, head_width)


def body(hidden, norm_gain, w_query, w_key, value_weight, vertical_blocks, slash_offsets, counts):
    features_all = lax.all_gather(hidden, "tp", axis=1, tiled=True)
    tok_rows = features_all.shape[0]
    widened = features_all.astype(jnp.float32)
    inv_rms = lax.rsqrt(jnp.mean(widened * widened, axis=-1, keepdims=True) + EPSILON)
    normed = (widened * inv_rms * norm_gain[None, :]).astype(jnp.bfloat16)
    head_width = w_key.shape[1]
    heads_here = w_query.shape[1] // head_width
    pieces = (
        lax.all_gather(w_query, "seq", axis=0, tiled=True),
        lax.all_gather(w_key, "seq", axis=0, tiled=True),
        lax.all_gather(value_weight, "seq", axis=0, tiled=True),
    )
    query_proj, key_projected, value_projected = tuple(
        (jnp.dot(normed, panel, preferred_element_type=jnp.float32) for panel in pieces)
    )
    device = lax.axis_index("seq")
    token_positions = device * tok_rows + jnp.arange(tok_rows, dtype=jnp.int32)
    queries = apply_rotary(
        query_proj.reshape(tok_rows, heads_here, head_width), token_positions, head_width
    ).astype(jnp.bfloat16)
    keys_here = (
        apply_rotary(key_projected.reshape(tok_rows, 1, head_width), token_positions, head_width)
        .reshape(tok_rows, head_width)
        .astype(jnp.bfloat16)
    )
    values_here = value_projected.astype(jnp.bfloat16)
    key_value_cache = jnp.stack([keys_here, values_here])
    keys_all, values_all = (
        lax.all_gather(keys_here, "seq", axis=0, tiled=True),
        lax.all_gather(values_here, "seq", axis=0, tiled=True),
    )
    group_base = lax.axis_index("tp") * heads_here
    block_count = tok_rows // BLOCK
    units = jnp.transpose(
        queries.reshape(block_count, BLOCK, heads_here, head_width), (2, 0, 1, 3)
    ).reshape(heads_here * block_count, BLOCK, head_width)
    local_starts = device * tok_rows + jnp.arange(block_count, dtype=jnp.int32) * BLOCK
    starts = jnp.tile(local_starts, heads_here)
    head_ids = group_base + jnp.repeat(jnp.arange(heads_here, dtype=jnp.int32), block_count)
    result = attend_all(
        units, starts, head_ids, keys_all, values_all, vertical_blocks, slash_offsets, counts
    )
    attn_out = jnp.transpose(
        result.reshape(heads_here, block_count, BLOCK, head_width), (1, 2, 0, 3)
    ).reshape(tok_rows, heads_here * head_width)
    return (attn_out, key_value_cache)


def solution(mesh):
    in_specs = (P("seq", "tp"), P(), P("seq", "tp"), P("seq", "tp"), P("seq", "tp"), P(), P(), P())
    out_specs = (P("seq", "tp"), P(None, "seq", "tp"))
    return jax.shard_map(body, mesh=mesh, in_specs=in_specs, out_specs=out_specs, check_vma=False)
```

profile of v0, /device:TPU:0, one launch (start us, length us, event | category | flops | bytes accessed | tf_op | source)
XLA Modules:
  0.0 516.6 jit_solution(12187914340762549450)
XLA Ops:
  7.2 0.7 all-gather.6.cloned.1.call-update
  8.0 0.7 all-gather.10.cloned.1.call-update
  8.7 0.7 all-gather.12.cloned.1.call-update
  9.4 0.5 all-gather.8.cloned.1.call-update
  10.2 0.5 multiply_cosine_fusion
  10.7 36.0 %all-gather.6.cloned.1.call-done = bf16[256,8192]{1,0:T(8,128)(2,1)} async-done(((bf16[256,2048]{1,0:T(8,128)(2,1)}), bf16[256,8192]{1,0:T(8,128)(2,1)}) %all-gather.6.cloned.1.call-update) | async-done | bytes 4194320 | tf_op jit(solution)/shard_map/all_gather | solution.py:105
  46.8 3.1 fusion.34
  49.9 48.1 %all-gather.10.cloned.1.call-done = bf16[8192,128]{1,0:T(8,128)(2,1)} async-done(((bf16[1024,128]{1,0:T(8,128)(2,1)}), bf16[8192,128]{1,0:T(8,128)(2,1)}) %all-gather.10.cloned.1.call-update) | async-done | bytes 2097168 | tf_op jit(solution)/shard_map/all_gather | solution.py:114
  98.0 4.6 convolution_bitcast_fusion.1
  102.6 0.3 fusion.41
  103.0 32.9 %all-gather = bf16[2048,1,128]{0,2,1:T(8,128)(2,1)S(1)} all-gather(bf16[256,1,128]{0,2,1:T(8,128)(2,1)S(1)} %maximum_convert_fusion), channel_id=2, replica_groups=mesh['seq'=8,'tp'=4] {'seq'}, dimensions={0}, use_global_device_ids=true | all-gather | bytes 589824 | tf_op jit(solution)/shard_map/all_gather | solution.py:133
  135.8 14.3 %all-gather.12.cloned.1.call-done = bf16[8192,128]{1,0:T(8,128)(2,1)} async-done(((bf16[1024,128]{1,0:T(8,128)(2,1)}), bf16[8192,128]{1,0:T(8,128)(2,1)}) %all-gather.12.cloned.1.call-update) | async-done | bytes 2097168 | tf_op jit(solution)/shard_map/all_gather | solution.py:115
  150.1 4.6 convolution_convert_fusion
  154.7 34.0 %all_gather.23 = bf16[2048,128]{0,1:T(8,128)(2,1)S(1)} all-gather(bf16[256,128]{0,1:T(8,128)(2,1)S(1)} %convolution_convert_fusion), channel_id=1, replica_groups=mesh['seq'=8,'tp'=4] {'seq'}, dimensions={0}, use_global_device_ids=true | all-gather | bytes 589824 | tf_op jit(solution)/shard_map/all_gather | solution.py:134
  188.9 0.5 copy.31
  189.4 0.8 copy.33
  190.2 191.3 %all-gather.8.cloned.1.call-done = bf16[8192,1024]{1,0:T(8,128)(2,1)} async-done(((bf16[1024,1024]{1,0:T(8,128)(2,1)}), bf16[8192,1024]{1,0:T(8,128)(2,1)}) %all-gather.8.cloned.1.call-update) | async-done | bytes 16777232 | tf_op jit(solution)/shard_map/all_gather | solution.py:113
  381.5 9.4 %convolution_bitcast_fusion = f32[32,8,8,128]{3,1,2,0:T(8,128)S(1)} fusion(bf16[8192,1024]{1,0:T(8,128)(2,1)} %all-gather.8.cloned.1.call-done, bf16[256,8192]{1,0:T(8,128)(2,1)} %all-gather.6.cloned.1.call-done, f32[8192]{0:T(1024)S(1)} %copy-done.3, f32[256]{0:T(256)S(1)} %add_rsqrt_fusion), kind=kOutput, calls=%fused_computation.53 | convolution fusion | flops 4303355904 | bytes 22053888 | tf_op jit(solution)/shard_map/dot_general | solution.py:118
  390.9 0.2 copy.35
  391.2 0.5 subtract_convert_fusion
  391.7 0.1 copy.28
  391.8 0.1 copy.29
  391.9 0.3 pad_maximum_fusion.1
  392.3 116.6 %while.12 = (s32[]{:T(128)}, bf16[4,8,64,128]{3,2,1,0:T(8,128)(2,1)S(1)}, s32[4,8]{1,0:T(4,128)S(1)}, s32[32,2]{0,1:T(2,128)S(1)}, s32[4,8]{1,0:T(4,128)S(1)}, /...) while((s32[]{:T(128)}, ...), condition=%wide.region_8.9_spmd, body=%wide.region_1.8_spmd.sunk | while | flops 551730432 | bytes 47082636 | solution.py:93
  392.4 0.4 select_reduce_fusion.5
  393.0 8.4 %gather_fusion = bf16[256,64,256]{2,1,0:T(8,128)(2,1)} fusion(bf16[32,64,256]{2,1,0:T(8,128)(2,1)S(1)} %get-tuple-element.277, s32[1024]{0:T(1024)S(1)} %pad_clamp_fusion.2), kind=kCustom, calls=%fused_computation.clone.1 | custom fusion | bytes 16778240 | tf_op jit(solution)/shard_map/while/body/eval_jaxpr/jit(_take)/gather | solution.py:61
  401.6 0.1 broadcast_in_dim.193
  401.7 8.0 %bitcast_select_fusion.2 = bf16[8,2048,256]{2,1,0:T(8,128)(2,1)} fusion(pred[8,2048]{1,0:T(8,128)(4,1)S(1)} %broadcast_in_dim.193, bf16[8,2048,256]{2,1,0:T(8,128)(2,1)} %bitcast.68), kind=kLoop, calls=%fused_computation.2.clone.1 | loop fusion | flops 4194304 | bytes 16793600 | tf_op jit(solution)/shard_map/while/body/eval_jaxpr/jit(_take)/select_n | solution.py:61
  409.7 0.1 select_reduce_fusion.6
  409.9 0.3 and_reduce_fusion.2
  410.4 0.1 broadcast_in_dim.194
  410.5 0.1 and.123
  411.1 6.6 %fusion.71 = (f32[8,64]{1,0:T(8,128)S(1)}, bf16[8,64,2048]{2,1,0:T(8,128)(2,1)}) fusion(s32[8,64]{1,0:T(8,128)S(1)} %iota_add_fusion.3, s32[8,2048]{1,0:T(8,128)S(1)} %broadcast_add_fusion.2, pred[8,2048]{1,0:T(8,128)(4,1)S(1)} %and.123, bf16[8,2048,256]{2,1,0:T(8,128)(2,1)} %bitcast_select_fusion.2, ...), kind=kOutput, calls=%fused_computation.78.clone.1 | convolution fusion | flops 278923264 | bytes 6597120 | tf_op jit(solution)/shard_map/while/body/eval_jaxpr/sub | solution.py:69
  417.7 3.7 fusion.72
  421.5 0.4 select_reduce_fusion.5
  422.1 8.4 %gather_fusion = bf16[256,64,256]{2,1,0:T(8,128)(2,1)} fusion(bf16[32,64,256]{2,1,0:T(8,128)(2,1)S(1)} %get-tuple-element.277, s32[1024]{0:T(1024)S(1)} %pad_clamp_fusion.2), kind=kCustom, calls=%fused_computation.clone.1 | custom fusion | bytes 16778240 | tf_op jit(solution)/shard_map/while/body/eval_jaxpr/jit(_take)/gather | solution.py:61
  430.7 0.1 broadcast_in_dim.193
  430.8 8.0 %bitcast_select_fusion.2 = bf16[8,2048,256]{2,1,0:T(8,128)(2,1)} fusion(pred[8,2048]{1,0:T(8,128)(4,1)S(1)} %broadcast_in_dim.193, bf16[8,2048,256]{2,1,0:T(8,128)(2,1)} %bitcast.68), kind=kLoop, calls=%fused_computation.2.clone.1 | loop fusion | flops 4194304 | bytes 16793600 | tf_op jit(solution)/shard_map/while/body/eval_jaxpr/jit(_take)/select_n | solution.py:61
  438.9 0.1 select_reduce_fusion.6
  439.1 0.3 and_reduce_fusion.2
  439.5 0.1 broadcast_in_dim.194
  439.7 0.1 and.123
  440.2 6.6 %fusion.71 = (f32[8,64]{1,0:T(8,128)S(1)}, bf16[8,64,2048]{2,1,0:T(8,128)(2,1)}) fusion(s32[8,64]{1,0:T(8,128)S(1)} %iota_add_fusion.3, s32[8,2048]{1,0:T(8,128)S(1)} %broadcast_add_fusion.2, pred[8,2048]{1,0:T(8,128)(4,1)S(1)} %and.123, bf16[8,2048,256]{2,1,0:T(8,128)(2,1)} %bitcast_select_fusion.2, ...), kind=kOutput, calls=%fused_computation.78.clone.1 | convolution fusion | flops 278923264 | bytes 6597120 | tf_op jit(solution)/shard_map/while/body/eval_jaxpr/sub | solution.py:69
  446.8 3.7 fusion.72
  450.6 0.4 select_reduce_fusion.5
  451.3 8.4 %gather_fusion = bf16[256,64,256]{2,1,0:T(8,128)(2,1)} fusion(bf16[32,64,256]{2,1,0:T(8,128)(2,1)S(1)} %get-tuple-element.277, s32[1024]{0:T(1024)S(1)} %pad_clamp_fusion.2), kind=kCustom, calls=%fused_computation.clone.1 | custom fusion | bytes 16778240 | tf_op jit(solution)/shard_map/while/body/eval_jaxpr/jit(_take)/gather | solution.py:61
  459.9 0.1 broadcast_in_dim.193
  460.0 8.0 %bitcast_select_fusion.2 = bf16[8,2048,256]{2,1,0:T(8,128)(2,1)} fusion(pred[8,2048]{1,0:T(8,128)(4,1)S(1)} %broadcast_in_dim.193, bf16[8,2048,256]{2,1,0:T(8,128)(2,1)} %bitcast.68), kind=kLoop, calls=%fused_computation.2.clone.1 | loop fusion | flops 4194304 | bytes 16793600 | tf_op jit(solution)/shard_map/while/body/eval_jaxpr/jit(_take)/select_n | solution.py:61
  468.0 0.1 select_reduce_fusion.6
  468.3 0.3 and_reduce_fusion.2
  468.8 0.1 and.123
  469.4 6.6 %fusion.71 = (f32[8,64]{1,0:T(8,128)S(1)}, bf16[8,64,2048]{2,1,0:T(8,128)(2,1)}) fusion(s32[8,64]{1,0:T(8,128)S(1)} %iota_add_fusion.3, s32[8,2048]{1,0:T(8,128)S(1)} %broadcast_add_fusion.2, pred[8,2048]{1,0:T(8,128)(4,1)S(1)} %and.123, bf16[8,2048,256]{2,1,0:T(8,128)(2,1)} %bitcast_select_fusion.2, ...), kind=kOutput, calls=%fused_computation.78.clone.1 | convolution fusion | flops 278923264 | bytes 6597120 | tf_op jit(solution)/shard_map/while/body/eval_jaxpr/sub | solution.py:69
  476.0 3.7 fusion.72
  479.8 0.4 select_reduce_fusion.5
  480.4 8.4 %gather_fusion = bf16[256,64,256]{2,1,0:T(8,128)(2,1)} fusion(bf16[32,64,256]{2,1,0:T(8,128)(2,1)S(1)} %get-tuple-element.277, s32[1024]{0:T(1024)S(1)} %pad_clamp_fusion.2), kind=kCustom, calls=%fused_computation.clone.1 | custom fusion | bytes 16778240 | tf_op jit(solution)/shard_map/while/body/eval_jaxpr/jit(_take)/gather | solution.py:61
  489.0 0.1 broadcast_in_dim.193
  489.1 8.0 %bitcast_select_fusion.2 = bf16[8,2048,256]{2,1,0:T(8,128)(2,1)} fusion(pred[8,2048]{1,0:T(8,128)(4,1)S(1)} %broadcast_in_dim.193, bf16[8,2048,256]{2,1,0:T(8,128)(2,1)} %bitcast.68), kind=kLoop, calls=%fused_computation.2.clone.1 | loop fusion | flops 4194304 | bytes 16793600 | tf_op jit(solution)/shard_map/while/body/eval_jaxpr/jit(_take)/select_n | solution.py:61
  497.2 0.1 select_reduce_fusion.6
  497.4 0.3 and_reduce_fusion.2
  498.0 0.1 and.123
  498.5 6.6 %fusion.71 = (f32[8,64]{1,0:T(8,128)S(1)}, bf16[8,64,2048]{2,1,0:T(8,128)(2,1)}) fusion(s32[8,64]{1,0:T(8,128)S(1)} %iota_add_fusion.3, s32[8,2048]{1,0:T(8,128)S(1)} %broadcast_add_fusion.2, pred[8,2048]{1,0:T(8,128)(4,1)S(1)} %and.123, bf16[8,2048,256]{2,1,0:T(8,128)(2,1)} %bitcast_select_fusion.2, ...), kind=kOutput, calls=%fused_computation.78.clone.1 | convolution fusion | flops 278923264 | bytes 6597120 | tf_op jit(solution)/shard_map/while/body/eval_jaxpr/sub | solution.py:69
  505.2 3.7 fusion.72
  508.9 0.3 copy.32
  509.2 0.9 copy.38
  (108 shorter events, 5.4 us)
Async XLA Ops:
  7.2 90.9 %copy-start.3 = (f32[8192]{0:T(1024)S(1)}, f32[8192]{0:T(1024)}, u32[]{:S(2)}) copy-start(f32[8192]{0:T(1024)} %param.11) | copy-start | bytes 98308
  7.2 39.6 %all-gather.6.cloned.1.call-start = ((), (), s32[]{:S(2)}) async-start(), calls=%async_computation | async-start | bytes 5242880 | tf_op jit(solution)/shard_map/all_gather | solution.py:105
  7.9 90.1 %all-gather.10.cloned.1.call-start = ((), (), s32[]{:S(2)}) async-start(), calls=%async_computation.2 | async-start | bytes 2359296 | tf_op jit(solution)/shard_map/all_gather | solution.py:114
  8.7 141.4 %all-gather.12.cloned.1.call-start = ((), (), s32[]{:S(2)}) async-start(), calls=%async_computation.3 | async-start | bytes 2359296 | tf_op jit(solution)/shard_map/all_gather | solution.py:115
  9.4 372.1 %all-gather.8.cloned.1.call-start = ((), (), s32[]{:S(2)}) async-start(), calls=%async_computation.1 | async-start | bytes 18874368 | tf_op jit(solution)/shard_map/all_gather | solution.py:113
  390.9 1.3 copy-start
  390.9 1.3 copy-start.1
  390.9 1.3 copy-start.2
Sparse Core Ops, SparseCore 0:
  9.5 37.1 all-gather.5
  48.9 49.0 all-gather.9
  100.1 49.9 all-gather.11
  152.1 229.3 all-gather.7
where the time goes:
time: 517 us
  waiting for transfers between devices  292 us (56%)
  blocking collectives  66.9 us (13%)
  matrix products  59.9 us (12%)
  other arithmetic  43 us (8%)
  local copies, waits for them, and re-layouts  40 us (8%)
  between operations  14 us (3%)
    all_gather x1, waiting for transfers between devices, body(): lax.all_gather(w_query, 'seq', axis=0, tiled=True)  191 us
    all_gather x1, waiting for transfers between devices, body(): lax.all_gather(w_key, 'seq', axis=0, tiled=True)  48.1 us
    all_gather x1, waiting for transfers between devices, body(): features_all = lax.all_gather(hidden, 'tp', axis=1, tiled=True)  36 us
    all_gather x1, blocking collectives, body(): lax.all_gather(values_here, 'seq', axis=0, tiled=True)  34 us
    gather x4, local copies, waits for them, and re-layouts, attend(): jnp.take(block_table, key_blocks, axis=0)  33.6 us
    all_gather x1, blocking collectives, body(): lax.all_gather(keys_here, 'seq', axis=0, tiled=True)  32.9 us
    select_n x8, other arithmetic, attend(): jnp.take(block_table, key_blocks, axis=0)  32.4 us
    sub x4, matrix products, attend(): weights = jnp.where(allowed, jnp.exp(masked - row_max), 0.0)  26.5 us
  transfers between devices with their start and end apart: 4, of which 4 were waited for; matrix products, arithmetic and copies ran while one was open for 3% of the time, Pallas kernels for 0%

commit v1 on v0

--- a/solution.py
+++ b/solution.py
@@ -102,7 +102,20 @@
 
 
 def body(hidden, norm_gain, w_query, w_key, value_weight, vertical_blocks, slash_offsets, counts):
-    features_all = lax.all_gather(hidden, "tp", axis=1, tiled=True)
+    before = lax.axis_size("tp")
+    lower, local_part, placed = (before, lax.axis_index("tp"), hidden.shape[1])
+    bank = tuple(((m, (m + 1) % lower) for m in range(lower)))
+    features_all = jnp.zeros(
+        (*hidden.shape[:1], lower * placed, *hidden.shape[1 + 1 :]), hidden.dtype
+    )
+    f_next = hidden
+    for k in range(lower):
+        part_now = (local_part - k) % lower
+        features_all = lax.dynamic_update_slice_in_dim(
+            features_all, f_next, part_now * placed, axis=1
+        )
+        if k < lower - 1:
+            f_next = lax.ppermute(f_next, "tp", bank)
     tok_rows = features_all.shape[0]
     widened = features_all.astype(jnp.float32)
     inv_rms = lax.rsqrt(jnp.mean(widened * widened, axis=-1, keepdims=True) + EPSILON)

time: 517 us -> 484 us (0.936)
  waiting for transfers between devices: 292 us -> 256 us
    all_gather x1, waiting for transfers between devices: 48.1 us -> 6 us  [body(): lax.all_gather(w_key, 'seq', axis=0, tiled=True)]
    ppermute x0 -> x3, waiting for transfers between devices: none -> 41.4 us  [body(): f_next = lax.ppermute(f_next, 'tp', bank)]
    all_gather x1 -> x0, waiting for transfers between devices: 36 us -> none  [body(): features_all = lax.all_gather(hidden, 'tp', axis=1, tiled=True)]
    all_gather x1, waiting for transfers between devices: 14.3 us -> 44.8 us  [body(): lax.all_gather(value_weight, 'seq', axis=0, tiled=True)]
    all_gather x1, waiting for transfers between devices: 191 us -> 161 us  [body(): lax.all_gather(w_query, 'seq', axis=0, tiled=True)]
  transfers between devices with their start and end apart: 4 -> 6, of which waited for: 4 -> 6; matrix products, arithmetic and copies ran while one was open for 3% -> 3% of each run, Pallas kernels for 0% -> 0%
where the time goes in v1:
time: 484 us; the launch traced here: 483 us
  waiting for transfers between devices  256 us (53%)
  blocking collectives  68.5 us (14%)
  matrix products  59.8 us (12%)
  local copies, waits for them, and re-layouts  43 us (9%)
  other arithmetic  40.9 us (8%)
  between operations  14 us (3%)
    all_gather x1, waiting for transfers between devices, body(): lax.all_gather(w_query, 'seq', axis=0, tiled=True)  161 us
    all_gather x1, waiting for transfers between devices, body(): lax.all_gather(value_weight, 'seq', axis=0, tiled=True)  44.8 us
    ppermute x3, waiting for transfers between devices, body(): f_next = lax.ppermute(f_next, 'tp', bank)  41.4 us
    all_gather x1, blocking collectives, body(): lax.all_gather(keys_here, 'seq', axis=0, tiled=True)  34.6 us
    all_gather x1, blocking collectives, body(): lax.all_gather(values_here, 'seq', axis=0, tiled=True)  33.9 us
    gather x4, local copies, waits for them, and re-layouts, attend(): jnp.take(block_table, key_blocks, axis=0)  33.7 us
    select_n x8, other arithmetic, attend(): jnp.take(block_table, key_blocks, axis=0)  32.4 us
    sub x4, matrix products, attend(): weights = jnp.where(allowed, jnp.exp(masked - row_max), 0.0)  26.5 us
  transfers between devices with their start and end apart: 6, of which 6 were waited for; matrix products, arithmetic and copies ran while one was open for 3% of the time, Pallas kernels for 0%

profile of v1, /device:TPU:0, one launch (start us, length us, event | category | flops | bytes accessed | tf_op | source)
XLA Modules:
  0.0 482.8 jit_solution(6131108125498336317)
XLA Ops:
  7.2 0.7 all-gather.7.cloned.1.call-update
  8.0 0.7 all-gather.9.cloned.1.call-update
  8.7 0.7 all-gather.5.cloned.1.call-update
  9.4 0.5 collective-permute-start
  9.9 14.6 %collective-permute-done = bf16[256,2048]{1,0:T(8,128)(2,1)S(1)} collective-permute-done((bf16[256,2048]{1,0:T(8,128)(2,1)}, bf16[256,2048]{1,0:T(8,128)(2,1)S(1)}, u32[]{:S(2)}, u32[]{:S(2)}) %collective-permute-start) | collective-permute-done | bytes 1048608 | tf_op jit(solution)/shard_map/ppermute | solution.py:118
  24.8 14.0 %collective-permute-done.1 = bf16[256,2048]{1,0:T(8,128)(2,1)S(1)} collective-permute-done((bf16[256,2048]{1,0:T(8,128)(2,1)S(1)}, bf16[256,2048]{1,0:T(8,128)(2,1)S(1)}, u32[]{:S(2)}, u32[]{:S(2)}) %collective-permute-start.1) | collective-permute-done | bytes 1048608 | tf_op jit(solution)/shard_map/ppermute | solution.py:118
  38.8 0.5 multiply_cosine_fusion
  39.4 0.5 broadcast_in_dim.158
  40.2 12.8 %collective-permute-done.2 = bf16[256,2048]{1,0:T(8,128)(2,1)S(1)} collective-permute-done((bf16[256,2048]{1,0:T(8,128)(2,1)S(1)}, bf16[256,2048]{1,0:T(8,128)(2,1)S(1)}, u32[]{:S(2)}, u32[]{:S(2)}) %collective-permute-start.2) | collective-permute-done | bytes 1048608 | tf_op jit(solution)/shard_map/ppermute | solution.py:118
  53.2 1.9 copy-done
  55.1 0.9 fusion.34
  56.0 6.0 %all-gather.7.cloned.1.call-done = bf16[8192,128]{1,0:T(8,128)(2,1)} async-done(((bf16[1024,128]{1,0:T(8,128)(2,1)}), bf16[8192,128]{1,0:T(8,128)(2,1)}) %all-gather.7.cloned.1.call-update) | async-done | bytes 2097168 | tf_op jit(solution)/shard_map/all_gather | solution.py:127
  62.0 4.6 convolution_bitcast_fusion.1
  66.6 0.3 fusion.41
  67.0 44.8 %all-gather.9.cloned.1.call-done = bf16[8192,128]{1,0:T(8,128)(2,1)} async-done(((bf16[1024,128]{1,0:T(8,128)(2,1)}), bf16[8192,128]{1,0:T(8,128)(2,1)}) %all-gather.9.cloned.1.call-update) | async-done | bytes 2097168 | tf_op jit(solution)/shard_map/all_gather | solution.py:128
  111.8 4.6 convolution_convert_fusion
  116.4 0.8 copy.33
  117.2 33.9 %all_gather.19 = bf16[2048,128]{0,1:T(8,128)(2,1)S(1)} all-gather(bf16[256,128]{0,1:T(8,128)(2,1)S(1)} %convolution_convert_fusion), channel_id=1, replica_groups=mesh['seq'=8,'tp'=4] {'seq'}, dimensions={0}, use_global_device_ids=true | all-gather | bytes 589824 | tf_op jit(solution)/shard_map/all_gather | solution.py:147
  151.1 34.6 %all-gather = bf16[2048,1,128]{0,2,1:T(8,128)(2,1)S(1)} all-gather(bf16[256,1,128]{0,2,1:T(8,128)(2,1)S(1)} %maximum_convert_fusion), channel_id=2, replica_groups=mesh['seq'=8,'tp'=4] {'seq'}, dimensions={0}, use_global_device_ids=true | all-gather | bytes 589824 | tf_op jit(solution)/shard_map/all_gather | solution.py:146
  185.8 0.5 copy.31
  186.3 161.3 %all-gather.5.cloned.1.call-done = bf16[8192,1024]{1,0:T(8,128)(2,1)} async-done(((bf16[1024,1024]{1,0:T(8,128)(2,1)}), bf16[8192,1024]{1,0:T(8,128)(2,1)}) %all-gather.5.cloned.1.call-update) | async-done | bytes 16777232 | tf_op jit(solution)/shard_map/all_gather | solution.py:126
  347.6 9.4 %convolution_bitcast_fusion = f32[32,8,8,128]{3,1,2,0:T(8,128)S(1)} fusion(bf16[8192,1024]{1,0:T(8,128)(2,1)} %all-gather.5.cloned.1.call-done, bf16[256,8192]{1,0:T(8,128)(2,1)} %copy-done, f32[8192]{0:T(1024)S(1)} %copy-done.6, f32[256]{0:T(256)S(1)} %add_rsqrt_fusion), kind=kOutput, calls=%fused_computation.53 | convolution fusion | flops 4303355904 | bytes 22053888 | tf_op jit(solution)/shard_map/dot_general | solution.py:131
  357.0 0.2 copy.35
  357.2 0.5 subtract_convert_fusion
  358.0 0.3 pad_maximum_fusion.1
  358.4 116.7 %while.12 = (s32[]{:T(128)}, bf16[4,8,64,128]{3,2,1,0:T(8,128)(2,1)S(1)}, s32[4,8]{1,0:T(4,128)S(1)}, s32[32,2]{0,1:T(2,128)S(1)}, s32[4,8]{1,0:T(4,128)S(1)}, /...) while((s32[]{:T(128)}, ...), condition=%wide.region_8.9_spmd, body=%wide.region_1.8_spmd.sunk | while | flops 551730432 | bytes 47082636 | solution.py:93
  358.5 0.4 select_reduce_fusion.5
  359.1 8.4 %gather_fusion = bf16[256,64,256]{2,1,0:T(8,128)(2,1)} fusion(bf16[32,64,256]{2,1,0:T(8,128)(2,1)S(1)} %get-tuple-element.277, s32[1024]{0:T(1024)S(1)} %pad_clamp_fusion.2), kind=kCustom, calls=%fused_computation.clone.1 | custom fusion | bytes 16778240 | tf_op jit(solution)/shard_map/while/body/eval_jaxpr/jit(_take)/gather | solution.py:61
  367.7 0.1 broadcast_in_dim.197
  367.8 8.0 %bitcast_select_fusion.2 = bf16[8,2048,256]{2,1,0:T(8,128)(2,1)} fusion(pred[8,2048]{1,0:T(8,128)(4,1)S(1)} %broadcast_in_dim.197, bf16[8,2048,256]{2,1,0:T(8,128)(2,1)} %bitcast.68), kind=kLoop, calls=%fused_computation.2.clone.1 | loop fusion | flops 4194304 | bytes 16793600 | tf_op jit(solution)/shard_map/while/body/eval_jaxpr/jit(_take)/select_n | solution.py:61
  375.8 0.1 select_reduce_fusion.6
  376.0 0.3 and_reduce_fusion.2
  376.6 0.1 and.144
  377.2 6.6 %fusion.71 = (f32[8,64]{1,0:T(8,128)S(1)}, bf16[8,64,2048]{2,1,0:T(8,128)(2,1)}) fusion(s32[8,64]{1,0:T(8,128)S(1)} %iota_add_fusion.3, s32[8,2048]{1,0:T(8,128)S(1)} %broadcast_add_fusion.2, pred[8,2048]{1,0:T(8,128)(4,1)S(1)} %and.144, bf16[8,2048,256]{2,1,0:T(8,128)(2,1)} %bitcast_select_fusion.2, ...), kind=kOutput, calls=%fused_computation.82.clone.1 | convolution fusion | flops 278923264 | bytes 6597120 | tf_op jit(solution)/shard_map/while/body/eval_jaxpr/sub | solution.py:69
  383.8 3.7 fusion.72
  387.6 0.4 select_reduce_fusion.5
  388.2 8.4 %gather_fusion = bf16[256,64,256]{2,1,0:T(8,128)(2,1)} fusion(bf16[32,64,256]{2,1,0:T(8,128)(2,1)S(1)} %get-tuple-element.277, s32[1024]{0:T(1024)S(1)} %pad_clamp_fusion.2), kind=kCustom, calls=%fused_computation.clone.1 | custom fusion | bytes 16778240 | tf_op jit(solution)/shard_map/while/body/eval_jaxpr/jit(_take)/gather | solution.py:61
  396.8 0.1 broadcast_in_dim.197
  397.0 8.0 %bitcast_select_fusion.2 = bf16[8,2048,256]{2,1,0:T(8,128)(2,1)} fusion(pred[8,2048]{1,0:T(8,128)(4,1)S(1)} %broadcast_in_dim.197, bf16[8,2048,256]{2,1,0:T(8,128)(2,1)} %bitcast.68), kind=kLoop, calls=%fused_computation.2.clone.1 | loop fusion | flops 4194304 | bytes 16793600 | tf_op jit(solution)/shard_map/while/body/eval_jaxpr/jit(_take)/select_n | solution.py:61
  405.0 0.1 select_reduce_fusion.6
  405.2 0.3 and_reduce_fusion.2
  405.8 0.1 and.144
  406.4 6.6 %fusion.71 = (f32[8,64]{1,0:T(8,128)S(1)}, bf16[8,64,2048]{2,1,0:T(8,128)(2,1)}) fusion(s32[8,64]{1,0:T(8,128)S(1)} %iota_add_fusion.3, s32[8,2048]{1,0:T(8,128)S(1)} %broadcast_add_fusion.2, pred[8,2048]{1,0:T(8,128)(4,1)S(1)} %and.144, bf16[8,2048,256]{2,1,0:T(8,128)(2,1)} %bitcast_select_fusion.2, ...), kind=kOutput, calls=%fused_computation.82.clone.1 | convolution fusion | flops 278923264 | bytes 6597120 | tf_op jit(solution)/shard_map/while/body/eval_jaxpr/sub | solution.py:69
  413.0 3.7 fusion.72
  416.8 0.4 select_reduce_fusion.5
  417.4 8.4 %gather_fusion = bf16[256,64,256]{2,1,0:T(8,128)(2,1)} fusion(bf16[32,64,256]{2,1,0:T(8,128)(2,1)S(1)} %get-tuple-element.277, s32[1024]{0:T(1024)S(1)} %pad_clamp_fusion.2), kind=kCustom, calls=%fused_computation.clone.1 | custom fusion | bytes 16778240 | tf_op jit(solution)/shard_map/while/body/eval_jaxpr/jit(_take)/gather | solution.py:61
  426.0 0.1 broadcast_in_dim.197
  426.2 8.0 %bitcast_select_fusion.2 = bf16[8,2048,256]{2,1,0:T(8,128)(2,1)} fusion(pred[8,2048]{1,0:T(8,128)(4,1)S(1)} %broadcast_in_dim.197, bf16[8,2048,256]{2,1,0:T(8,128)(2,1)} %bitcast.68), kind=kLoop, calls=%fused_computation.2.clone.1 | loop fusion | flops 4194304 | bytes 16793600 | tf_op jit(solution)/shard_map/while/body/eval_jaxpr/jit(_take)/select_n | solution.py:61
  434.2 0.1 select_reduce_fusion.6
  434.4 0.3 and_reduce_fusion.2
  435.0 0.1 and.144
  435.6 6.6 %fusion.71 = (f32[8,64]{1,0:T(8,128)S(1)}, bf16[8,64,2048]{2,1,0:T(8,128)(2,1)}) fusion(s32[8,64]{1,0:T(8,128)S(1)} %iota_add_fusion.3, s32[8,2048]{1,0:T(8,128)S(1)} %broadcast_add_fusion.2, pred[8,2048]{1,0:T(8,128)(4,1)S(1)} %and.144, bf16[8,2048,256]{2,1,0:T(8,128)(2,1)} %bitcast_select_fusion.2, ...), kind=kOutput, calls=%fused_computation.82.clone.1 | convolution fusion | flops 278923264 | bytes 6597120 | tf_op jit(solution)/shard_map/while/body/eval_jaxpr/sub | solution.py:69
  442.2 3.7 fusion.72
  446.0 0.4 select_reduce_fusion.5
  446.6 8.4 %gather_fusion = bf16[256,64,256]{2,1,0:T(8,128)(2,1)} fusion(bf16[32,64,256]{2,1,0:T(8,128)(2,1)S(1)} %get-tuple-element.277, s32[1024]{0:T(1024)S(1)} %pad_clamp_fusion.2), kind=kCustom, calls=%fused_computation.clone.1 | custom fusion | bytes 16778240 | tf_op jit(solution)/shard_map/while/body/eval_jaxpr/jit(_take)/gather | solution.py:61
  455.2 0.1 broadcast_in_dim.197
  455.3 8.0 %bitcast_select_fusion.2 = bf16[8,2048,256]{2,1,0:T(8,128)(2,1)} fusion(pred[8,2048]{1,0:T(8,128)(4,1)S(1)} %broadcast_in_dim.197, bf16[8,2048,256]{2,1,0:T(8,128)(2,1)} %bitcast.68), kind=kLoop, calls=%fused_computation.2.clone.1 | loop fusion | flops 4194304 | bytes 16793600 | tf_op jit(solution)/shard_map/while/body/eval_jaxpr/jit(_take)/select_n | solution.py:61
  463.4 0.1 select_reduce_fusion.6
  463.6 0.3 and_reduce_fusion.2
  464.2 0.1 and.144
  464.7 6.6 %fusion.71 = (f32[8,64]{1,0:T(8,128)S(1)}, bf16[8,64,2048]{2,1,0:T(8,128)(2,1)}) fusion(s32[8,64]{1,0:T(8,128)S(1)} %iota_add_fusion.3, s32[8,2048]{1,0:T(8,128)S(1)} %broadcast_add_fusion.2, pred[8,2048]{1,0:T(8,128)(4,1)S(1)} %and.144, bf16[8,2048,256]{2,1,0:T(8,128)(2,1)} %bitcast_select_fusion.2, ...), kind=kOutput, calls=%fused_computation.82.clone.1 | convolution fusion | flops 278923264 | bytes 6597120 | tf_op jit(solution)/shard_map/while/body/eval_jaxpr/sub | solution.py:69
  471.3 3.7 fusion.72
  475.0 0.3 copy.32
  475.4 0.9 copy.38
  (122 shorter events, 6.4 us)
Async XLA Ops:
  7.2 32.7 %copy-start.1 = (bf16[256,2048]{1,0:T(8,128)(2,1)S(1)}, bf16[256,2048]{1,0:T(8,128)(2,1)}, u32[]{:S(2)}) copy-start(bf16[256,2048]{1,0:T(8,128)(2,1)} %param.10) | copy-start | bytes 3145732
  7.2 54.8 %all-gather.7.cloned.1.call-start = ((), (), s32[]{:S(2)}) async-start(), calls=%async_computation.1 | async-start | bytes 2359296 | tf_op jit(solution)/shard_map/all_gather | solution.py:127
  7.9 103.9 %all-gather.9.cloned.1.call-start = ((), (), s32[]{:S(2)}) async-start(), calls=%async_computation.2 | async-start | bytes 2359296 | tf_op jit(solution)/shard_map/all_gather | solution.py:128
  8.7 338.9 %all-gather.5.cloned.1.call-start = ((), (), s32[]{:S(2)}) async-start(), calls=%async_computation | async-start | bytes 18874368 | tf_op jit(solution)/shard_map/all_gather | solution.py:126
  9.4 15.2 %collective-permute-start = (bf16[256,2048]{1,0:T(8,128)(2,1)}, bf16[256,2048]{1,0:T(8,128)(2,1)S(1)}, u32[]{:S(2)}, u32[]{:S(2)}) collective-permute-start(bf16[256,2048]{1,0:T(8,128)(2,1)} %param.10), channel_id=1, source_target_pairs={{0,1},{1,2},{2,3},{3,0},{4,5},{5,6},{6,7},{7,4},{8,9},{9,10},{10,1... | collective-permute-start | bytes 3145736 | tf_op jit(solution)/shard_map/ppermute | solution.py:118
  24.6 14.2 %collective-permute-start.1 = (bf16[256,2048]{1,0:T(8,128)(2,1)S(1)}, bf16[256,2048]{1,0:T(8,128)(2,1)S(1)}, u32[]{:S(2)}, u32[]{:S(2)}) collective-permute-start(bf16[256,2048]{1,0:T(8,128)(2,1)S(1)} %collective-permute-done), channel_id=1, source_target_pairs={{0,1},{1,2},{2,3},{3,0},{4,5},{5,6},{6,7},{7,4},{8,9},{9,10},{10,1... | collective-permute-start | bytes 3145736 | tf_op jit(solution)/shard_map/ppermute | solution.py:118
  38.8 14.2 %collective-permute-start.2 = (bf16[256,2048]{1,0:T(8,128)(2,1)S(1)}, bf16[256,2048]{1,0:T(8,128)(2,1)S(1)}, u32[]{:S(2)}, u32[]{:S(2)}) collective-permute-start(bf16[256,2048]{1,0:T(8,128)(2,1)S(1)} %collective-permute-done.1), channel_id=1, source_target_pairs={{0,1},{1,2},{2,3},{3,0},{4,5},{5,6},{6,7},{7,4},{8,9},{9,10},{10,1... | collective-permute-start | bytes 3145736 | tf_op jit(solution)/shard_map/ppermute | solution.py:118
  40.1 21.9 %copy-start.6 = (f32[8192]{0:T(1024)S(1)}, f32[8192]{0:T(1024)}, u32[]{:S(2)}) copy-start(f32[8192]{0:T(1024)} %param.11) | copy-start | bytes 98308
  53.1 1.9 copy-start
  357.0 1.3 copy-start.2
  357.0 1.3 copy-start.3
  357.0 1.3 copy-start.4
  357.0 1.3 copy-start.5
Sparse Core Ops, SparseCore 0:
  10.1 51.8 all-gather.6
  64.1 47.6 all-gather.8
  113.9 233.6 all-gather.4
